TPU v7x, 32 devices: a whole 2x2x4 slice. The times are simulated.
32 devices in a mesh: row: 8 (over z, x), col: 2 (over y), depth: 2 (over core).
Axes of the slice: x: 2, y: 2, z: 4, core: 2. Of those that a mesh axis runs over, the one named last changes fastest.
Arguments:
- volume: bfloat16 [16, 32, 16, 256], P('row', 'col', 'depth'), may hold values from -6 to 6
- first_kernel: bfloat16 [27, 256, 256], P(None, 'row'), may hold values from -0.078125 to 0.078125
- down_kernel: bfloat16 [8, 256, 512], replicated, may hold values from -0.125 to 0.125
- mid_kernel: bfloat16 [27, 512, 512], P(None, None, 'col'), may hold values from -0.0546875 to 0.0546875
- up_kernel: bfloat16 [8, 512, 256], replicated, may hold values from -0.25 to 0.25
- last_kernel: bfloat16 [27, 512, 256], P(None, 'row'), may hold values from -0.0546875 to 0.0546875
Outputs:
- decoded: bfloat16 [16, 32, 16, 256], P('row', 'col', 'depth')
All inputs are finite; a program needn't handle non-finite values.
Results may differ from a plain program's by a relative error of at most 0.0055.
Values may be sent and summed in bfloat16 or wider, within the bound.
A program may use at most 64 MiB of HBM per device.

v0:
```python
import jax
import jax.numpy as jnp
from jax import lax
from jax.sharding import PartitionSpec as P


def padded(cells, sides, width):
    for axis, dim in sides:
        count = lax.axis_size(axis)
        ends = count - 1
        head = lax.slice_in_dim(cells, 0, width, axis=dim)
        tail = lax.slice_in_dim(cells, cells.shape[dim] - width, cells.shape[dim], axis=dim)
        cells = jnp.concatenate(
            [
                lax.ppermute(tail, axis, [(i, (i + 1) % count) for i in range(ends)]),
                cells,
                lax.ppermute(head, axis, [((i + 1) % count, i) for i in range(ends)]),
            ],
            axis=dim,
        )
    return cells


def tap_adder(framed, running, weights_part):
    out_x = framed.shape[0] - 2
    out_y = framed.shape[1] - 2
    out_z = framed.shape[2] - 2
    in_count = weights_part.shape[1]
    windows = []
    for kernel_tap in range(27):
        shift_x = kernel_tap // 9
        shift_y = kernel_tap // 3 % 3
        shift_z = kernel_tap % 3
        window = framed[
            shift_x : shift_x + out_x, shift_y : shift_y + out_y, shift_z : shift_z + out_z
        ]
        windows.append(window.reshape(-1, in_count))
    if in_count < 512:
        stacked = jnp.concatenate(windows, axis=1)
        flat_weights = weights_part.reshape(27 * in_count, weights_part.shape[2])
        return jnp.dot(stacked, flat_weights, preferred_element_type=jnp.float32)
    for kernel_tap in range(27):
        running = running + jnp.dot(
            windows[kernel_tap], weights_part[kernel_tap], preferred_element_type=jnp.float32
        )
    return running


def body(volume, first_kernel, down_kernel, mid_kernel, up_kernel, last_kernel):
    size_x, size_y, size_z, channels = volume.shape
    half_x, half_y, half_z = (size_x // 2, size_y // 2, size_z // 2)
    wide_chans = down_kernel.shape[2]
    framed_fine = padded(volume, (("row", 0), ("col", 1), ("depth", 2)), 1)
    zero_fine = jnp.zeros((size_x * size_y * size_z, first_kernel.shape[2]), jnp.float32)
    first_sum = tap_adder(
        framed_fine, zero_fine, lax.all_gather(first_kernel, "row", axis=1, tiled=True)
    )
    skip = jax.nn.gelu(first_sum).astype(jnp.bfloat16).reshape(size_x, size_y, size_z, channels)
    blocks = skip.reshape(half_x, 2, half_y, 2, half_z, 2, channels)
    blocks = jnp.transpose(blocks, (0, 2, 4, 1, 3, 5, 6)).reshape(-1, 8 * channels)
    coarse_sum = jnp.dot(
        blocks, down_kernel.reshape(8 * channels, wide_chans), preferred_element_type=jnp.float32
    )
    coarse = (
        jax.nn.gelu(coarse_sum).astype(jnp.bfloat16).reshape(half_x, half_y, half_z, wide_chans)
    )
    slab_cells = lax.all_gather(coarse, "col", axis=1, tiled=True)
    framed_slab = padded(slab_cells, (("row", 0), ("depth", 2)), 1)
    framed_slab = jnp.pad(framed_slab, ((0, 0), (1, 1), (0, 0), (0, 0)))
    slab_cols = framed_slab.shape[1] - 2
    zero_slab = jnp.zeros((half_x * slab_cols * half_z, mid_kernel.shape[2]), jnp.float32)
    middle_sum = tap_adder(framed_slab, zero_slab, mid_kernel)
    middle = (
        jax.nn.gelu(middle_sum)
        .astype(jnp.bfloat16)
        .reshape(half_x, slab_cols, half_z, mid_kernel.shape[2])
    )
    every_channel = lax.all_gather(middle, "col", axis=3, tiled=True)
    own_cells = lax.dynamic_slice_in_dim(every_channel, lax.axis_index("col") * half_y, half_y, 1)
    up_table = jnp.transpose(up_kernel, (1, 0, 2)).reshape(wide_chans, 8 * channels)
    lifted_flat = jnp.dot(
        own_cells.reshape(-1, wide_chans), up_table, preferred_element_type=jnp.float32
    ).astype(jnp.bfloat16)
    lifted = lifted_flat.reshape(half_x, half_y, half_z, 2, 2, 2, channels)
    lifted = jnp.transpose(lifted, (0, 3, 1, 4, 2, 5, 6)).reshape(size_x, size_y, size_z, channels)
    joined = jnp.concatenate([lifted, skip], axis=-1)
    framed_joined = padded(joined, (("row", 0), ("col", 1), ("depth", 2)), 1)
    zero_last = jnp.zeros((size_x * size_y * size_z, last_kernel.shape[2]), jnp.float32)
    last_sum = tap_adder(
        framed_joined, zero_last, lax.all_gather(last_kernel, "row", axis=1, tiled=True)
    )
    return (
        jax.nn.gelu(last_sum)
        .astype(jnp.bfloat16)
        .reshape(size_x, size_y, size_z, last_kernel.shape[2])
    )


def solution(mesh):
    placed = (
        P("row", "col", "depth", None),
        P(None, "row", None),
        P(),
        P(None, None, "col"),
        P(),
        P(None, "row", None),
    )
    return jax.shard_map(
        body, mesh=mesh, in_specs=placed, out_specs=P("row", "col", "depth", None), check_vma=False
    )
```

profile of v0, /device:TPU:0, one launch (start us, length us, event | category | flops | bytes accessed | tf_op | source)
XLA Modules:
  0.0 216.9 jit_solution(18109129788605676376)
XLA Ops:
  8.2 4.9 %collective-permute-start = (bf16[1,16,8,256]{3,2,1,0:T(8,128)(2,1)S(1)}, bf16[1,16,8,256]{3,2,1,0:T(8,128)(2,1)S(1)}, u32[]{:S(2)}, u32[]{:S(2)}) collective-permute-start(bf16[1,16,8,256]{3,2,1,0:T(8,128)(2,1)S(1)} %get-tuple-element.107), channel_id=1, source_target_pairs={{0,4},{4,8},{8,12},{12,16},{16,20},{20,24},{24,28},{1,5},{5,9},{9,... | collective-permute-start | bytes 196616 | tf_op jit(solution)/shard_map/ppermute | solution.py:15
  15.0 4.3 %collective-permute-done.1 = bf16[1,16,8,256]{3,2,1,0:T(8,128)(2,1)S(1)} collective-permute-done((bf16[1,16,8,256]{3,2,1,0:T(8,128)(2,1)S(1)}, bf16[1,16,8,256]{3,2,1,0:T(8,128)(2,1)S(1)}, u32[]{:S(2)}, u32[]{:S(2)}) %collective-permute-start.1) | collective-permute-done | bytes 65568 | tf_op jit(solution)/shard_map/ppermute | solution.py:17
  20.3 3.4 %collective-permute-start.2 = (bf16[4,1,8,256]{3,2,1,0:T(8,128)(2,1)S(1)}, bf16[4,1,8,256]{3,2,1,0:T(8,128)(2,1)S(1)}, u32[]{:S(2)}, u32[]{:S(2)}) collective-permute-start(bf16[4,1,8,256]{3,2,1,0:T(8,128)(2,1)S(1)} %get-tuple-element.96), channel_id=1, source_target_pairs={{0,2},{1,3},{4,6},{5,7},{8,10},{9,11},{12,14},{13,15},{16,18},{17,... | collective-permute-start | bytes 49160 | tf_op jit(solution)/shard_map/ppermute | solution.py:15
  25.0 3.9 %copy.13 = bf16[8,512,256]{1,2,0:T(8,128)(2,1)} copy(bf16[8,512,256]{2,1,0:T(8,128)(2,1)} %param.10) | data formatting | bytes 4194304 | tf_op args[4]
  29.4 1.3 collective-permute-start.4
  32.1 1.8 collective-permute-done.5
  53.1 23.8 %all-gather.3.cloned.1.call-done = bf16[27,256,256]{2,1,0:T(8,128)(2,1)} async-done(((bf16[27,32,256]{2,1,0:T(8,128)(2,1)}), bf16[27,256,256]{2,1,0:T(8,128)(2,1)}) %all-gather.3.cloned.1.call-update) | async-done | bytes 3538960 | tf_op jit(solution)/shard_map/all_gather | solution.py:56
  76.9 4.2 %fusion.40 = bf16[256,256]{1,0:T(8,128)(2,1)S(1)} fusion(bf16[256,6912]{1,0:T(8,128)(2,1)} %constant_dynamic-update-slice_fusion.3, bf16[6912,256]{1,0:T(8,128)(2,1)} %bitcast.411), kind=kOutput, calls=%fused_computation.80 | convolution fusion | flops 906559488 | bytes 7208960 | tf_op jit(solution)/shard_map/dot_general | solution.py:41
  81.8 4.6 %all_gather.13 = bf16[1,16,4,512]{3,2,0,1:T(4,128)(2,1)S(1)} all-gather(bf16[1,8,4,512]{3,2,0,1:T(4,128)(2,1)S(1)} %bitcast.410), channel_id=1, replica_groups=mesh['row'=8,'col'=2,'depth'=2] {'col'}, dimensions={1}, use_global_device_ids=true | all-gather | bytes 98304 | tf_op jit(solution)/shard_map/all_gather | solution.py:67
  86.4 2.5 %collective-permute-start.6 = (bf16[1,16,4,512]{3,2,0,1:T(4,128)(2,1)S(1)}, bf16[1,16,4,512]{3,2,0,1:T(4,128)(2,1)S(1)}, u32[]{:S(2)}, u32[]{:S(2)}) collective-permute-start(bf16[1,16,4,512]{3,2,0,1:T(4,128)(2,1)S(1)} %all_gather.13), channel_id=1, source_target_pairs={{0,4},{4,8},{8,12},{12,16},{16,20},{20,24},{24,28},{1,5},{5,9},{9,... | collective-permute-start | bytes 196616 | tf_op jit(solution)/shard_map/ppermute | solution.py:15
  90.2 1.8 fusion.89
  92.4 4.6 %collective-permute-done.7 = bf16[1,16,4,512]{3,2,0,1:T(4,128)(2,1)S(1)} collective-permute-done((bf16[1,16,4,512]{3,2,0,1:T(4,128)(2,1)S(1)}, bf16[1,16,4,512]{3,2,0,1:T(4,128)(2,1)S(1)}, u32[]{:S(2)}, u32[]{:S(2)}) %collective-permute-start.7) | collective-permute-done | bytes 65568 | tf_op jit(solution)/shard_map/ppermute | solution.py:17
  97.1 1.3 collective-permute-start.8
  99.8 1.7 fusion.101
  101.5 1.7 fusion.78
  109.7 1.5 reshape.321
  111.2 1.5 reshape.323
  115.9 1.5 reshape.332
  147.1 4.8 %all_gather.14 = bf16[1,16,4,512]{3,2,1,0:T(4,128)(2,1)S(1)} all-gather(bf16[1,16,4,256]{3,2,1,0:T(4,128)(2,1)S(1)} %reshape.336), channel_id=1, replica_groups=mesh['row'=8,'col'=2,'depth'=2] {'col'}, dimensions={3}, use_global_device_ids=true | all-gather | bytes 98304 | tf_op jit(solution)/shard_map/all_gather | solution.py:78
  152.0 2.3 %convolution_convert_fusion = bf16[32,2048]{1,0:T(8,128)(2,1)S(1)} fusion(bf16[32,512]{1,0:T(8,128)(2,1)S(1)} %reshape.337, bf16[512,2048]{0,1:T(8,128)(2,1)} %bitcast.347), kind=kOutput, calls=%fused_computation | convolution fusion | flops 67174400 | bytes 2260992 | tf_op jit(solution)/shard_map/dot_general | solution.py:81
  154.6 6.2 %collective-permute-start.10 = (bf16[1,16,8,512]{3,2,1,0:T(8,128)(2,1)S(1)}, bf16[1,16,8,512]{3,2,1,0:T(8,128)(2,1)S(1)}, u32[]{:S(2)}, u32[]{:S(2)}) collective-permute-start(bf16[1,16,8,512]{3,2,1,0:T(8,128)(2,1)S(1)} %get-tuple-element.91), channel_id=1, source_target_pairs={{0,4},{4,8},{8,12},{12,16},{16,20},{20,24},{24,28},{1,5},{5,9},{9,... | collective-permute-start | bytes 393224 | tf_op jit(solution)/shard_map/ppermute | solution.py:15
  162.8 5.5 %collective-permute-done.10 = bf16[1,16,8,512]{3,2,1,0:T(8,128)(2,1)S(1)} collective-permute-done((bf16[1,16,8,512]{3,2,1,0:T(8,128)(2,1)S(1)}, bf16[1,16,8,512]{3,2,1,0:T(8,128)(2,1)S(1)}, u32[]{:S(2)}, u32[]{:S(2)}) %collective-permute-start.10) | collective-permute-done | bytes 131104 | tf_op jit(solution)/shard_map/ppermute | solution.py:15
  168.3 3.6 %collective-permute-start.12 = (bf16[4,1,8,512]{3,2,1,0:T(8,128)(2,1)S(1)}, bf16[4,1,8,512]{3,2,1,0:T(8,128)(2,1)S(1)}, u32[]{:S(2)}, u32[]{:S(2)}) collective-permute-start(bf16[4,1,8,512]{3,2,1,0:T(8,128)(2,1)S(1)} %get-tuple-element.53), channel_id=1, source_target_pairs={{0,2},{1,3},{4,6},{5,7},{8,10},{9,11},{12,14},{13,15},{16,18},{17,... | collective-permute-start | bytes 98312 | tf_op jit(solution)/shard_map/ppermute | solution.py:15
  174.1 3.6 %collective-permute-done.13 = bf16[4,1,8,512]{3,2,1,0:T(8,128)(2,1)S(1)} collective-permute-done((bf16[4,1,8,512]{3,2,1,0:T(8,128)(2,1)S(1)}, bf16[4,1,8,512]{3,2,1,0:T(8,128)(2,1)S(1)}, u32[]{:S(2)}, u32[]{:S(2)}) %collective-permute-start.13) | collective-permute-done | bytes 32800 | tf_op jit(solution)/shard_map/ppermute | solution.py:17
  177.9 1.3 collective-permute-start.14
  179.2 1.5 collective-permute-start.15
  185.1 1.6 fusion.161
  186.7 5.0 %all-gather.5.cloned.1.call-done = bf16[27,512,256]{2,1,0:T(8,128)(2,1)} async-done(((bf16[27,64,256]{2,1,0:T(8,128)(2,1)}), bf16[27,512,256]{2,1,0:T(8,128)(2,1)}) %all-gather.5.cloned.1.call-update) | async-done | bytes 7077904 | tf_op jit(solution)/shard_map/all_gather | solution.py:90
  191.7 1.4 fusion.65
  193.1 1.8 fusion.63
  194.9 1.3 fusion.64
  200.2 1.3 fusion.68
  (193 shorter events, 91.3 us)
Async XLA Ops:
  6.5 74.8 %copy-start = (bf16[8,256,512]{2,1,0:T(8,128)(2,1)S(1)}, bf16[8,256,512]{2,1,0:T(8,128)(2,1)}, u32[]{:S(2)}) copy-start(bf16[8,256,512]{2,1,0:T(8,128)(2,1)} %param.8) | copy-start | bytes 6291460
  6.5 70.3 %all-gather.3.cloned.1.call-start = ((), (), s32[]{:S(2)}) async-start(), calls=%async_computation | async-start | bytes 3981312 | tf_op jit(solution)/shard_map/all_gather | solution.py:56
  7.3 184.4 %all-gather.5.cloned.1.call-start = ((), (), s32[]{:S(2)}) async-start(), calls=%async_computation.1 | async-start | bytes 7962624 | tf_op jit(solution)/shard_map/all_gather | solution.py:90
  8.2 6.8 %collective-permute-start = (bf16[1,16,8,256]{3,2,1,0:T(8,128)(2,1)S(1)}, bf16[1,16,8,256]{3,2,1,0:T(8,128)(2,1)S(1)}, u32[]{:S(2)}, u32[]{:S(2)}) collective-permute-start(bf16[1,16,8,256]{3,2,1,0:T(8,128)(2,1)S(1)} %get-tuple-element.107), channel_id=1, source_target_pairs={{0,4},{4,8},{8,12},{12,16},{16,20},{20,24},{24,28},{1,5},{5,9},{9,... | collective-permute-start | bytes 196616 | tf_op jit(solution)/shard_map/ppermute | solution.py:15
  13.1 6.2 %collective-permute-start.1 = (bf16[1,16,8,256]{3,2,1,0:T(8,128)(2,1)S(1)}, bf16[1,16,8,256]{3,2,1,0:T(8,128)(2,1)S(1)}, u32[]{:S(2)}, u32[]{:S(2)}) collective-permute-start(bf16[1,16,8,256]{3,2,1,0:T(8,128)(2,1)S(1)} %get-tuple-element.106), channel_id=1, source_target_pairs={{4,0},{8,4},{12,8},{16,12},{20,16},{24,20},{28,24},{5,1},{9,5},{13... | collective-permute-start | bytes 196616 | tf_op jit(solution)/shard_map/ppermute | solution.py:17
  20.3 8.7 %collective-permute-start.2 = (bf16[4,1,8,256]{3,2,1,0:T(8,128)(2,1)S(1)}, bf16[4,1,8,256]{3,2,1,0:T(8,128)(2,1)S(1)}, u32[]{:S(2)}, u32[]{:S(2)}) collective-permute-start(bf16[4,1,8,256]{3,2,1,0:T(8,128)(2,1)S(1)} %get-tuple-element.96), channel_id=1, source_target_pairs={{0,2},{1,3},{4,6},{5,7},{8,10},{9,11},{12,14},{13,15},{16,18},{17,... | collective-permute-start | bytes 49160 | tf_op jit(solution)/shard_map/ppermute | solution.py:15
  23.7 5.6 %collective-permute-start.3 = (bf16[4,1,8,256]{3,2,1,0:T(8,128)(2,1)S(1)}, bf16[4,1,8,256]{3,2,1,0:T(8,128)(2,1)S(1)}, u32[]{:S(2)}, u32[]{:S(2)}) collective-permute-start(bf16[4,1,8,256]{3,2,1,0:T(8,128)(2,1)S(1)} %get-tuple-element.97), channel_id=1, source_target_pairs={{2,0},{3,1},{6,4},{7,5},{10,8},{11,9},{14,12},{15,13},{18,16},{19,... | collective-permute-start | bytes 49160 | tf_op jit(solution)/shard_map/ppermute | solution.py:17
  29.4 2.7 %collective-permute-start.4 = (bf16[4,18,1,256]{3,2,1,0:T(2,128)(2,1)S(1)}, bf16[4,18,1,256]{3,2,1,0:T(2,128)(2,1)S(1)}, u32[]{:S(2)}, u32[]{:S(2)}) collective-permute-start(bf16[4,18,1,256]{3,2,1,0:T(2,128)(2,1)S(1)} %get-tuple-element.82), channel_id=1, source_target_pairs={{0,1},{2,3},{4,5},{6,7},{8,9},{10,11},{12,13},{14,15},{16,17},{18,... | collective-permute-start | bytes 110600 | tf_op jit(solution)/shard_map/ppermute | solution.py:15
  30.7 3.2 %collective-permute-start.5 = (bf16[4,18,1,256]{3,2,1,0:T(2,128)(2,1)S(1)}, bf16[4,18,1,256]{3,2,1,0:T(2,128)(2,1)S(1)}, u32[]{:S(2)}, u32[]{:S(2)}) collective-permute-start(bf16[4,18,1,256]{3,2,1,0:T(2,128)(2,1)S(1)} %get-tuple-element.81), channel_id=1, source_target_pairs={{1,0},{3,2},{5,4},{7,6},{9,8},{11,10},{13,12},{15,14},{17,16},{19,... | collective-permute-start | bytes 110600 | tf_op jit(solution)/shard_map/ppermute | solution.py:17
  34.3 9.2 %copy-start.2 = (bf16[2,16,8,256]{3,2,1,0:T(8,128)(2,1)S(1)}, bf16[2,16,8,256]{3,2,1,0:T(8,128)(2,1)}, u32[]{:S(2)}) copy-start(bf16[2,16,8,256]{3,2,1,0:T(8,128)(2,1)} %param.6) | copy-start | bytes 393220
  86.4 5.9 %collective-permute-start.6 = (bf16[1,16,4,512]{3,2,0,1:T(4,128)(2,1)S(1)}, bf16[1,16,4,512]{3,2,0,1:T(4,128)(2,1)S(1)}, u32[]{:S(2)}, u32[]{:S(2)}) collective-permute-start(bf16[1,16,4,512]{3,2,0,1:T(4,128)(2,1)S(1)} %all_gather.13), channel_id=1, source_target_pairs={{0,4},{4,8},{8,12},{12,16},{16,20},{20,24},{24,28},{1,5},{5,9},{9,... | collective-permute-start | bytes 196616 | tf_op jit(solution)/shard_map/ppermute | solution.py:15
  88.9 8.1 %collective-permute-start.7 = (bf16[1,16,4,512]{3,2,0,1:T(4,128)(2,1)S(1)}, bf16[1,16,4,512]{3,2,0,1:T(4,128)(2,1)S(1)}, u32[]{:S(2)}, u32[]{:S(2)}) collective-permute-start(bf16[1,16,4,512]{3,2,0,1:T(4,128)(2,1)S(1)} %all_gather.13), channel_id=1, source_target_pairs={{4,0},{8,4},{12,8},{16,12},{20,16},{24,20},{28,24},{5,1},{9,5},{13... | collective-permute-start | bytes 196616 | tf_op jit(solution)/shard_map/ppermute | solution.py:17
  97.1 6.1 %collective-permute-start.8 = (bf16[3,16,1,512]{3,2,0,1:T(2,128)(2,1)S(1)}, bf16[3,16,1,512]{3,2,0,1:T(2,128)(2,1)S(1)}, u32[]{:S(2)}, u32[]{:S(2)}) collective-permute-start(bf16[3,16,1,512]{3,2,0,1:T(2,128)(2,1)S(1)} %get-tuple-element.101), channel_id=1, source_target_pairs={{0,1},{2,3},{4,5},{6,7},{8,9},{10,11},{12,13},{14,15},{16,17},{18,... | collective-permute-start | bytes 147464 | tf_op jit(solution)/shard_map/ppermute | solution.py:15
  98.4 4.8 %collective-permute-start.9 = (bf16[3,16,1,512]{3,2,0,1:T(2,128)(2,1)S(1)}, bf16[3,16,1,512]{3,2,0,1:T(2,128)(2,1)S(1)}, u32[]{:S(2)}, u32[]{:S(2)}) collective-permute-start(bf16[3,16,1,512]{3,2,0,1:T(2,128)(2,1)S(1)} %get-tuple-element.102), channel_id=1, source_target_pairs={{1,0},{3,2},{5,4},{7,6},{9,8},{11,10},{13,12},{15,14},{17,16},{19,... | collective-permute-start | bytes 147464 | tf_op jit(solution)/shard_map/ppermute | solution.py:17
  115.9 13.1 %copy-start.16 = (f32[64,256]{1,0:T(8,128)S(1)}, f32[64,256]{1,0:T(8,128)}, u32[]{:S(2)}) copy-start(f32[64,256]{1,0:T(8,128)} %fusion.101) | copy-start | bytes 196612
  126.7 17.0 %copy-start.15 = (f32[64,256]{1,0:T(8,128)S(1)}, f32[64,256]{1,0:T(8,128)}, u32[]{:S(2)}) copy-start(f32[64,256]{1,0:T(8,128)} %fusion.78) | copy-start | bytes 196612
  130.1 15.9 %copy-start.17 = (bf16[64,512]{1,0:T(8,128)(2,1)S(1)}, bf16[64,512]{1,0:T(8,128)(2,1)}, u32[]{:S(2)}) copy-start(bf16[64,512]{1,0:T(8,128)(2,1)} %reshape.335) | copy-start | bytes 196612
  154.6 13.7 %collective-permute-start.10 = (bf16[1,16,8,512]{3,2,1,0:T(8,128)(2,1)S(1)}, bf16[1,16,8,512]{3,2,1,0:T(8,128)(2,1)S(1)}, u32[]{:S(2)}, u32[]{:S(2)}) collective-permute-start(bf16[1,16,8,512]{3,2,1,0:T(8,128)(2,1)S(1)} %get-tuple-element.91), channel_id=1, source_target_pairs={{0,4},{4,8},{8,12},{12,16},{16,20},{20,24},{24,28},{1,5},{5,9},{9,... | collective-permute-start | bytes 393224 | tf_op jit(solution)/shard_map/ppermute | solution.py:15
  160.8 7.5 %collective-permute-start.11 = (bf16[1,16,8,512]{3,2,1,0:T(8,128)(2,1)S(1)}, bf16[1,16,8,512]{3,2,1,0:T(8,128)(2,1)S(1)}, u32[]{:S(2)}, u32[]{:S(2)}) collective-permute-start(bf16[1,16,8,512]{3,2,1,0:T(8,128)(2,1)S(1)} %get-tuple-element.92), channel_id=1, source_target_pairs={{4,0},{8,4},{12,8},{16,12},{20,16},{24,20},{28,24},{5,1},{9,5},{13... | collective-permute-start | bytes 393224 | tf_op jit(solution)/shard_map/ppermute | solution.py:17
  168.3 5.8 %collective-permute-start.12 = (bf16[4,1,8,512]{3,2,1,0:T(8,128)(2,1)S(1)}, bf16[4,1,8,512]{3,2,1,0:T(8,128)(2,1)S(1)}, u32[]{:S(2)}, u32[]{:S(2)}) collective-permute-start(bf16[4,1,8,512]{3,2,1,0:T(8,128)(2,1)S(1)} %get-tuple-element.53), channel_id=1, source_target_pairs={{0,2},{1,3},{4,6},{5,7},{8,10},{9,11},{12,14},{13,15},{16,18},{17,... | collective-permute-start | bytes 98312 | tf_op jit(solution)/shard_map/ppermute | solution.py:15
  171.9 5.8 %collective-permute-start.13 = (bf16[4,1,8,512]{3,2,1,0:T(8,128)(2,1)S(1)}, bf16[4,1,8,512]{3,2,1,0:T(8,128)(2,1)S(1)}, u32[]{:S(2)}, u32[]{:S(2)}) collective-permute-start(bf16[4,1,8,512]{3,2,1,0:T(8,128)(2,1)S(1)} %get-tuple-element.54), channel_id=1, source_target_pairs={{2,0},{3,1},{6,4},{7,5},{10,8},{11,9},{14,12},{15,13},{18,16},{19,... | collective-permute-start | bytes 98312 | tf_op jit(solution)/shard_map/ppermute | solution.py:17
  177.9 4.8 %collective-permute-start.14 = (bf16[4,18,1,512]{3,2,1,0:T(2,128)(2,1)S(1)}, bf16[4,18,1,512]{3,2,1,0:T(2,128)(2,1)S(1)}, u32[]{:S(2)}, u32[]{:S(2)}) collective-permute-start(bf16[4,18,1,512]{3,2,1,0:T(2,128)(2,1)S(1)} %get-tuple-element.26), channel_id=1, source_target_pairs={{0,1},{2,3},{4,5},{6,7},{8,9},{10,11},{12,13},{14,15},{16,17},{18,... | collective-permute-start | bytes 221192 | tf_op jit(solution)/shard_map/ppermute | solution.py:15
  179.2 3.5 %collective-permute-start.15 = (bf16[4,18,1,512]{3,2,1,0:T(2,128)(2,1)S(1)}, bf16[4,18,1,512]{3,2,1,0:T(2,128)(2,1)S(1)}, u32[]{:S(2)}, u32[]{:S(2)}) collective-permute-start(bf16[4,18,1,512]{3,2,1,0:T(2,128)(2,1)S(1)} %get-tuple-element.25), channel_id=1, source_target_pairs={{1,0},{3,2},{5,4},{7,6},{9,8},{11,10},{13,12},{15,14},{17,16},{19,... | collective-permute-start | bytes 221192 | tf_op jit(solution)/shard_map/ppermute | solution.py:17
  191.7 12.4 %copy-start.1 = (bf16[27,512,256]{2,1,0:T(8,128)(2,1)S(1)}, bf16[27,512,256]{2,1,0:T(8,128)(2,1)}, u32[]{:S(2)}) copy-start(bf16[27,512,256]{2,1,0:T(8,128)(2,1)} %all-gather.5.cloned.1.call-done) | copy-start | bytes 21233668
  193.1 12.1 %copy-start.5 = (bf16[2,16,8,512]{3,2,1,0:T(8,128)(2,1)S(1)}, bf16[2,16,8,512]{3,2,1,0:T(8,128)(2,1)}, u32[]{:S(2)}) copy-start(bf16[2,16,8,512]{3,2,1,0:T(8,128)(2,1)} %get-tuple-element.19) | copy-start | bytes 786436
  194.9 10.5 %copy-start.4 = (bf16[2,16,8,512]{3,2,1,0:T(8,128)(2,1)S(1)}, bf16[2,16,8,512]{3,2,1,0:T(8,128)(2,1)}, u32[]{:S(2)}) copy-start(bf16[2,16,8,512]{3,2,1,0:T(8,128)(2,1)} %get-tuple-element.18) | copy-start | bytes 786436
  196.3 9.4 %copy-start.8 = (bf16[2,16,8,512]{3,2,1,0:T(8,128)(2,1)S(1)}, bf16[2,16,8,512]{3,2,1,0:T(8,128)(2,1)}, u32[]{:S(2)}) copy-start(bf16[2,16,8,512]{3,2,1,0:T(8,128)(2,1)} %get-tuple-element.50) | copy-start | bytes 786436
  198.8 7.3 %copy-start.10 = (bf16[2,16,8,512]{3,2,1,0:T(8,128)(2,1)S(1)}, bf16[2,16,8,512]{3,2,1,0:T(8,128)(2,1)}, u32[]{:S(2)}) copy-start(bf16[2,16,8,512]{3,2,1,0:T(8,128)(2,1)} %get-tuple-element.46) | copy-start | bytes 786436
  200.1 6.3 %copy-start.6 = (bf16[2,16,8,512]{3,2,1,0:T(8,128)(2,1)S(1)}, bf16[2,16,8,512]{3,2,1,0:T(8,128)(2,1)}, u32[]{:S(2)}) copy-start(bf16[2,16,8,512]{3,2,1,0:T(8,128)(2,1)} %get-tuple-element.90) | copy-start | bytes 786436
  201.5 5.2 %copy-start.3 = (bf16[2,16,8,512]{3,2,1,0:T(8,128)(2,1)S(1)}, bf16[2,16,8,512]{3,2,1,0:T(8,128)(2,1)}, u32[]{:S(2)}) copy-start(bf16[2,16,8,512]{3,2,1,0:T(8,128)(2,1)} %get-tuple-element.6) | copy-start | bytes 786436
  205.2 2.2 %copy-start.7 = (bf16[2,16,8,512]{3,2,1,0:T(8,128)(2,1)S(1)}, bf16[2,16,8,512]{3,2,1,0:T(8,128)(2,1)}, u32[]{:S(2)}) copy-start(bf16[2,16,8,512]{3,2,1,0:T(8,128)(2,1)} %get-tuple-element.49) | copy-start | bytes 786436
  206.2 1.7 copy-start.13
  (4 other events, 4.8 us)
Sparse Core Ops, SparseCore 0:
  9.5 67.3 all-gather.2
  79.1 112.5 all-gather.4
where the time goes:
time: 219 us; the launch traced here: 217 us
  matrix products  57.7 us (26%)
  waiting for transfers between devices  50.7 us (23%)
  local copies, waits for them, and re-layouts  44.6 us (20%)
  starting transfers between devices  35 us (16%)
  between operations  14.3 us (7%)
  blocking collectives  9.39 us (4%)
  other arithmetic  5.38 us (2%)
    dot_general x54, matrix products, tap_adder(): jnp.dot(windows[kernel_tap], weights_part[kernel_tap], preferred_element_...  50.7 us
    ppermute x8, starting transfers between devices, padded(): lax.ppermute(tail, axis, [(i, (i + 1) % count) for i in range(ends)])  24.4 us
    all_gather x1, waiting for transfers between devices, body(): lax.all_gather(first_kernel, 'row', axis=1, tiled=True)  23.8 us
    unnamed x66, local copies, waits for them, and re-layouts  22 us
    ppermute x8, waiting for transfers between devices, padded(): lax.ppermute(head, axis, [((i + 1) % count, i) for i in range(ends)])  14.6 us
    reshape x27, local copies, waits for them, and re-layouts, tap_adder(): windows.append(window.reshape(-1, in_count))  13.7 us
    ppermute x8, starting transfers between devices, padded(): lax.ppermute(head, axis, [((i + 1) % count, i) for i in range(ends)])  10.5 us
    ppermute x8, waiting for transfers between devices, padded(): lax.ppermute(tail, axis, [(i, (i + 1) % count) for i in range(ends)])  6.47 us
  transfers between devices with their start and end apart: 18, of which 10 were waited for; matrix products, arithmetic and copies ran while one was open for 41% of the time, Pallas kernels for 0%

commit v1 on v0

v1 whole, which is shorter than its diff:
```python
import functools

import jax
import jax.numpy as jnp
from jax import lax
from jax.experimental import pallas as pl
from jax.experimental.pallas import tpu as pltpu
from jax.sharding import PartitionSpec as P

MESH = pl.DeviceIdType.MESH
BF = jnp.bfloat16
F32 = jnp.float32


def gelu(v):
    return jax.nn.gelu(v, approximate=True)


def dot(a, b):
    return jnp.dot(a, b, preferred_element_type=F32)


def z_shifted(v, shift):
    if shift == 0:
        return v
    depth = v.shape[-2]
    rolled = pltpu.roll(v, (-shift) % depth, axis=v.ndim - 2)
    at = lax.broadcasted_iota(jnp.int32, v.shape, v.ndim - 2)
    edge = depth - 1 if shift > 0 else 0
    return jnp.where(at == edge, 0.0, rolled)


def kernel(
    sizes,
    vol_ref, first_ref, down_hbm, mid_hbm, up_hbm, last_ref,
    out_ref,
    vol_pair, vol_taps, first_w, last_w, down_ref, mid_ref, up_ref,
    joined, joined_taps, acc, coarse_pad, coarse_own, coarse_taps,
    middle_out, middle_all, piece_out, piece_all,
    local_sem, w_send, w_recv, relay_send, relay_recv,
    halo_send, halo_recv, pair_send, pair_recv,
    coarse_send, coarse_recv, mid_send, mid_recv,
):
    R, Q, D = sizes
    r, q, c = lax.axis_index("row"), lax.axis_index("col"), lax.axis_index("depth")
    X, Y, Z, C = vol_ref.shape
    ZF = Z * D
    half = C // D
    hx, hy, hz = X // 2, Y // 2, ZF // 2
    wide = down_hbm.shape[2]
    wm = mid_hbm.shape[2]
    group = 9
    parity = q % 2
    lane0 = pl.multiple_of(c * half, half)

    def remote(src, dst, ssem, rsem, dev):
        return pltpu.make_async_remote_copy(
            src_ref=src, dst_ref=dst, send_sem=ssem, recv_sem=rsem,
            device_id=dev, device_id_type=MESH,
        )

    local = [
        pltpu.make_async_copy(down_hbm, down_ref, local_sem.at[0]),
        pltpu.make_async_copy(mid_hbm, mid_ref, local_sem.at[1]),
        pltpu.make_async_copy(up_hbm, up_ref, local_sem.at[2]),
    ]
    shards = []
    for slot, (shard, gathered) in enumerate(((first_ref, first_w), (last_ref, last_w))):
        rows = shard.shape[1]
        own = pl.ds(pl.multiple_of(r * rows, rows), rows)
        shards.append(pltpu.make_async_copy(
            shard.at[:, :, pl.ds(lane0, half)], gathered.at[:, own, :], local_sem.at[3 + slot]))
    zero_c = jnp.zeros(vol_pair.shape[1:], BF)
    for d in range(D):
        vol_pair[d] = zero_c
    joined[...] = jnp.zeros(joined.shape, BF)
    coarse_pad[...] = jnp.zeros(coarse_pad.shape, BF)
    vol_pair[c, 1:X + 1, 1:Y + 1] = vol_ref[...]

    barrier = pltpu.get_barrier_semaphore()
    for k in range(1, R):
        pl.semaphore_signal(barrier, inc=1, device_id=((r + k) % R, q, c), device_id_type=MESH)
    for k in range(1, D):
        pl.semaphore_signal(barrier, inc=1, device_id=(r, q, (c + k) % D), device_id_type=MESH)
    for dx in (-1, 0, 1):
        for k in range(1, Q):
            def greet(dx=dx, k=k):
                pl.semaphore_signal(
                    barrier, inc=1, device_id=(r + dx, (q + k) % Q, c), device_id_type=MESH)
            if dx == 0:
                greet()
            else:
                pl.when((r + dx >= 0) & (r + dx < R))(greet)
    sides = jnp.where(r > 0, 1, 0) + jnp.where(r < R - 1, 1, 0)
    pl.semaphore_wait(barrier, (R - 1) + (D - 1) + (1 + sides) * (Q - 1))

    for copy in local + shards:
        copy.start()

    def halo(buf, lanes, slot, start):
        n = 0
        for dx in (-1, 0, 1):
            for dy in (-1, 0, 1):
                if dx == 0 and dy == 0:
                    continue
                sx = {1: pl.ds(X, 1), -1: pl.ds(1, 1), 0: pl.ds(1, X)}[dx]
                tx = {1: pl.ds(0, 1), -1: pl.ds(X + 1, 1), 0: pl.ds(1, X)}[dx]
                sy = {1: pl.ds(Y, 1), -1: pl.ds(1, 1), 0: pl.ds(1, Y)}[dy]
                ty = {1: pl.ds(0, 1), -1: pl.ds(Y + 1, 1), 0: pl.ds(1, Y)}[dy]
                copy = remote(
                    buf.at[sx, sy, :, lanes], buf.at[tx, ty, :, lanes],
                    halo_send.at[slot, n], halo_recv.at[slot, n], (r + dx, q + dy, c))
                to = (r + dx >= 0) & (r + dx < R) & (q + dy >= 0) & (q + dy < Q)
                come = (r - dx >= 0) & (r - dx < R) & (q - dy >= 0) & (q - dy < Q)
                if start:
                    pl.when(to)(copy.start)
                else:
                    pl.when(come)(copy.wait_recv)
                    pl.when(to)(copy.wait_send)
                n += 1

    everything = pl.ds(0, C)
    halo(vol_pair.at[c], everything, 0, True)

    def spread(shard, gathered, slot):
        rows = shard.shape[1]
        own = pl.ds(pl.multiple_of(r * rows, rows), rows)
        taps = pl.ds(group * parity, 2 * group)
        return [
            remote(
                shard.at[taps, :, pl.ds(lane0, half)], gathered.at[taps, own, :],
                w_send.at[slot, k], w_recv.at[slot, k], ((r + k) % R, q, c))
            for k in range(1, R)
        ]

    def relays(shard, gathered, slot):
        rows = shard.shape[1]
        taps = pl.ds(2 * group * parity, group)
        other = q + 1 - 2 * parity
        out = []
        for k in range(1, R):
            origin = (r + R - k) % R
            at = pl.ds(pl.multiple_of(origin * rows, rows), rows)
            out.append(remote(
                gathered.at[taps, at, :], gathered.at[taps, at, :],
                relay_send.at[slot, k], relay_recv.at[slot, k], (r, other, c)))
        return out

    first_out, last_out = spread(first_ref, first_w, 0), spread(last_ref, last_w, 1)
    first_relay, last_relay = relays(first_ref, first_w, 0), relays(last_ref, last_w, 1)
    for copy in first_out:
        copy.start()

    halo(vol_pair.at[c], everything, 0, False)

    def pair_copy(src, dst, slot, k):
        return remote(src, dst, pair_send.at[slot, k], pair_recv.at[slot, k], (r, q, (c + k) % D))

    vols = [pair_copy(vol_pair.at[c], vol_pair.at[c], 0, k) for k in range(1, D)]
    for copy in vols:
        copy.start()
    for copy in vols:
        copy.wait_recv()

    def build_taps(get, taps_ref, chans, width):
        for x in range(taps_ref.shape[0]):
            v = get(x)
            for s in range(3):
                taps_ref[x, :, :, s * width + chans.start:s * width + chans.stop] = (
                    z_shifted(v, s - 1).astype(taps_ref.dtype))

    def vol_plane(x):
        return jnp.concatenate([vol_pair[d, x].astype(F32) for d in range(D)], axis=1)

    build_taps(vol_plane, vol_taps, slice(0, C), C)

    for copy, relay in zip(first_out, first_relay):
        copy.wait_recv()
        relay.start()
    for copy in last_out:
        copy.start()
    shards[0].wait()
    for relay in first_relay:
        relay.wait_recv()

    def conv(taps_ref, weights):
        chans = weights.shape[1]
        for ab in range(9):
            a, b = ab // 3, ab % 3
            rhs = weights[3 * ab:3 * ab + 3].reshape(3 * chans, weights.shape[2])
            for x in range(X):
                lhs = taps_ref[x + a, b:b + Y].reshape(Y * ZF, 3 * chans)
                part = dot(lhs, rhs)
                if ab == 0:
                    acc[x] = part
                else:
                    acc[x] += part

    conv(vol_taps, first_w)
    skip_lanes = pl.ds(pl.multiple_of(C + c * half, half), half)
    for x in range(X):
        joined[x + 1, 1:Y + 1, :, skip_lanes] = gelu(acc[x]).astype(BF).reshape(Y, ZF, half)
    inside = joined.at[pl.ds(1, X), pl.ds(1, Y), :, skip_lanes]
    skips = [pair_copy(inside, inside, 1, k) for k in range(1, D)]
    for copy in skips:
        copy.start()
    for copy in skips:
        copy.wait_recv()
    upper = pl.ds(C, C)
    halo(joined, upper, 1, True)

    local[0].wait()
    fine_rows, coarse_rows = hy * ZF, hy * hz
    rows_c = lax.broadcasted_iota(jnp.int32, (coarse_rows, fine_rows), 0)
    rows_f = lax.broadcasted_iota(jnp.int32, (coarse_rows, fine_rows), 1)
    pick = [jnp.where(rows_f == 2 * rows_c + s, 1.0, 0.0).astype(BF) for s in range(2)]
    for i in range(hx):
        total = jnp.zeros((coarse_rows, wide), F32)
        for a in range(2):
            for b in range(2):
                rows = jnp.concatenate(
                    [joined[1 + 2 * i + a, 1 + 2 * j + b, :, C:2 * C] for j in range(hy)], axis=0)
                for s in range(2):
                    picked = dot(pick[s], rows).astype(BF)
                    total += dot(picked, down_ref[4 * a + 2 * b + s])
        coarse_own[i] = gelu(total).reshape(hy, hz, wide).astype(BF)

    sends = []
    for dx in (-1, 0, 1):
        src = {1: pl.ds(hx - 1, 1), -1: pl.ds(0, 1), 0: pl.ds(0, hx)}[dx]
        dst = {1: pl.ds(0, 1), -1: pl.ds(hx + 1, 1), 0: pl.ds(1, hx)}[dx]
        for k in range(Q):
            if dx == 0 and k == 0:
                continue
            at = pl.ds(1 + q * hy, hy)
            copy = remote(
                coarse_own.at[src], coarse_pad.at[dst, at],
                coarse_send.at[dx + 1, k], coarse_recv.at[dx + 1, k], (r + dx, (q + k) % Q, c))
            to = (r + dx >= 0) & (r + dx < R)
            come = (r - dx >= 0) & (r - dx < R)
            sends.append((dx, copy, to, come))
    for dx, copy, to, come in sends:
        if dx == 0:
            copy.start()
        else:
            pl.when(to)(copy.start)
    coarse_pad[1:1 + hx, pl.ds(1 + q * hy, hy)] = coarse_own[...]
    for dx, copy, to, come in sends:
        if dx == 0:
            copy.wait_recv()
        else:
            pl.when(come)(copy.wait_recv)
    build_taps(lambda x: coarse_pad[x].astype(F32), coarse_taps, slice(0, wide), wide)

    local[1].wait()
    slab = Q * hy
    for i in range(hx):
        total = jnp.zeros((slab * hz, wm), F32)
        for ab in range(9):
            a, b = ab // 3, ab % 3
            lhs = coarse_taps[i + a, b:b + slab].reshape(slab * hz, 3 * wide).astype(BF)
            total += dot(lhs, mid_ref[3 * ab:3 * ab + 3].reshape(3 * wide, wm))
        middle = gelu(total).astype(BF)
        for part in range(Q):
            middle_out[part, i] = middle[part * coarse_rows:(part + 1) * coarse_rows]
    mids = []
    for k in range(1, Q):
        target = (q + k) % Q
        mids.append(remote(
            middle_out.at[target], middle_all.at[q], mid_send.at[k], mid_recv.at[k],
            (r, target, c)))
    for copy in mids:
        copy.start()
    middle_all[q] = middle_out[q]

    for copy, relay in zip(last_out, last_relay):
        copy.wait_recv()
        relay.start()

    halo(joined, upper, 1, False)
    for x in range(X + 2):
        v = joined[x, :, :, C:2 * C].astype(F32)
        for s in range(3):
            joined_taps[x, :, :, s * 2 * C + C:(s + 1) * 2 * C] = z_shifted(v, s - 1).astype(BF)

    for copy in mids:
        copy.wait_recv()
    local[2].wait()
    rows_f = lax.broadcasted_iota(jnp.int32, (fine_rows, coarse_rows), 0)
    rows_c = lax.broadcasted_iota(jnp.int32, (fine_rows, coarse_rows), 1)
    place = [jnp.where(rows_f == 2 * rows_c + s, 1.0, 0.0).astype(BF) for s in range(2)]
    for i in range(hx):
        spread_rows = [
            [dot(place[s], middle_all[part, i]).astype(BF) for s in range(2)] for part in range(Q)]
        for a in range(2):
            for b in range(2):
                lifted = jnp.zeros((fine_rows, C), F32)
                for part in range(Q):
                    for s in range(2):
                        lifted += dot(
                            spread_rows[part][s],
                            up_ref[4 * a + 2 * b + s, part * wm:(part + 1) * wm])
                lifted = lifted.astype(BF)
                for j in range(hy):
                    joined[1 + 2 * i + a, 1 + 2 * j + b, :, 0:C] = lifted[j * ZF:(j + 1) * ZF]
    lower = pl.ds(0, C)
    halo(joined, lower, 2, True)
    shards[1].wait()
    for relay in last_relay:
        relay.wait_recv()
    halo(joined, lower, 2, False)
    for x in range(X + 2):
        v = joined[x, :, :, 0:C].astype(F32)
        for s in range(3):
            joined_taps[x, :, :, s * 2 * C:s * 2 * C + C] = z_shifted(v, s - 1).astype(BF)

    conv(joined_taps, last_w)
    for x in range(X):
        done = gelu(acc[x]).reshape(Y, D, Z, half)
        for d in range(D):
            piece_out[d, x] = done[:, d].astype(BF)
    pieces = []
    for k in range(1, D):
        target = (c + k) % D
        pieces.append(pair_copy(piece_out.at[target], piece_all.at[c], 2, k))
    for copy in pieces:
        copy.start()
    piece_all[c] = piece_out[c]
    for copy in pieces:
        copy.wait_recv()
    for d in range(D):
        out_ref[:, :, :, d * half:(d + 1) * half] = piece_all[d]

    for copy in first_out + last_out + first_relay + last_relay + vols + skips + mids + pieces:
        copy.wait_send()
    for dx, copy, to, come in sends:
        if dx == 0:
            copy.wait_send()
        else:
            pl.when(to)(copy.wait_send)


def body(sizes, volume, first_kernel, down_kernel, mid_kernel, up_kernel, last_kernel):
    R, Q, D = sizes
    X, Y, Z, C = volume.shape
    ZF, half = Z * D, C // D
    hx, hy, hz = X // 2, Y // 2, ZF // 2
    wide, wm = down_kernel.shape[2], mid_kernel.shape[2]
    slab = Q * hy
    DMA = pltpu.SemaphoreType.DMA
    vmem = pl.BlockSpec(memory_space=pltpu.VMEM)
    hbm = pl.BlockSpec(memory_space=pl.ANY)
    return pl.pallas_call(
        functools.partial(kernel, sizes),
        out_shape=jax.ShapeDtypeStruct(volume.shape, BF),
        in_specs=[vmem] + [hbm] * 5,
        out_specs=vmem,
        scratch_shapes=[
            pltpu.VMEM((D, X + 2, Y + 2, Z, C), BF),
            pltpu.VMEM((X + 2, Y + 2, ZF, 3 * C), BF),
            pltpu.VMEM((27, C, half), BF),
            pltpu.VMEM((27, 2 * C, half), BF),
            pltpu.VMEM(down_kernel.shape, BF),
            pltpu.VMEM(mid_kernel.shape, BF),
            pltpu.VMEM(up_kernel.shape, BF),
            pltpu.VMEM((X + 2, Y + 2, ZF, 2 * C), BF),
            pltpu.VMEM((X + 2, Y + 2, ZF, 6 * C), BF),
            pltpu.VMEM((X, Y * ZF, half), F32),
            pltpu.VMEM((hx + 2, slab + 2, hz, wide), BF),
            pltpu.VMEM((hx, hy, hz, wide), BF),
            pltpu.VMEM((hx + 2, slab + 2, hz, 3 * wide), F32),
            pltpu.VMEM((Q, hx, hy * hz, wm), BF),
            pltpu.VMEM((Q, hx, hy * hz, wm), BF),
            pltpu.VMEM((D, X, Y, Z, half), BF),
            pltpu.VMEM((D, X, Y, Z, half), BF),
            DMA((5,)),
            DMA((2, R)), DMA((2, R)), DMA((2, R)), DMA((2, R)),
            DMA((3, 8)), DMA((3, 8)),
            DMA((3, D)), DMA((3, D)),
            DMA((3, Q)), DMA((3, Q)),
            DMA((Q,)), DMA((Q,)),
        ],
        compiler_params=pltpu.CompilerParams(
            collective_id=0, has_side_effects=True, vmem_limit_bytes=60 * 1024 * 1024),
        name="unet",
    )(volume, first_kernel, down_kernel, mid_kernel, up_kernel, last_kernel)


def solution(mesh):
    sizes = tuple(mesh.shape[name] for name in ("row", "col", "depth"))
    placed = (
        P("row", "col", "depth", None),
        P(None, "row", None),
        P(),
        P(None, None, "col"),
        P(),
        P(None, "row", None),
    )
    return jax.shard_map(
        functools.partial(body, sizes), mesh=mesh, in_specs=placed,
        out_specs=P("row", "col", "depth", None), check_vma=False,
    )
```

time: 219 us -> 125 us (0.57)
  the two profiles are of different devices: /device:TPU:0 before, /device:TPU:15 now
where the time goes in v1:
time: 125 us
  Pallas kernels  124 us (99%)
  local copies, waits for them, and re-layouts  1.57 us (1%)
    pallas_call x1, Pallas kernels, body(): pl.pallas_call(functools.partial(kernel, sizes), out_shape=jax.ShapeDtype...  124 us

profile of v1, /device:TPU:15, one launch (start us, length us, event | category | flops | bytes accessed | tf_op | source)
XLA Modules:
  0.0 125.1 jit_solution(9509328824216472394)
XLA Ops:
  0.0 123.6 %unet.1 = bf16[2,16,8,256]{3,2,1,0:T(8,128)(2,1)} custom-call(bf16[2,16,8,256]{3,2,1,0:T(8,128)(2,1)} %vol_ref.1, bf16[27,32,256]{2,1,0:T(8,128)(2,1)} %first_ref.1, bf16[8,256,512]{2,1,0:T(8,128)(2,1)} %down_hbm.1, bf16[27,512,256]{2,1,0:T(8,128)(2,1)} %mid_hbm.1, bf16[8,512,256]{2,1,0:T(8,128)(2,1)} %up_hbm.1, bf16[27,64,256]{2,1,0:T(8,128)(2,1)} %last_ref.1), custom_call_target="tpu_custom_call" | custom-call | tf_op jit(solution)/shard_map/unet/pallas_call | solution.py:353
  123.6 1.6 %copy.8 = bf16[2,16,8,256]{3,2,1,0:T(8,128)(2,1)} copy(bf16[2,16,8,256]{3,2,1,0:T(8,128)(2,1)} %unet.1) | data formatting | bytes 262144

commit v2 on v1

--- a/solution.py
+++ b/solution.py
@@ -37,7 +37,7 @@
     vol_pair, vol_taps, first_w, last_w, down_ref, mid_ref, up_ref,
     joined, joined_taps, acc, coarse_pad, coarse_own, coarse_taps,
     middle_out, middle_all, piece_out, piece_all,
-    local_sem, w_send, w_recv, relay_send, relay_recv,
+    local_sem, w_send, w_recv, x_send, x_recv, relay_send, relay_recv,
     halo_send, halo_recv, pair_send, pair_recv,
     coarse_send, coarse_recv, mid_send, mid_recv,
 ):
@@ -122,34 +122,71 @@
     everything = pl.ds(0, C)
     halo(vol_pair.at[c], everything, 0, True)
 
-    def spread(shard, gathered, slot):
-        rows = shard.shape[1]
-        own = pl.ds(pl.multiple_of(r * rows, rows), rows)
-        taps = pl.ds(group * parity, 2 * group)
-        return [
-            remote(
-                shard.at[taps, :, pl.ds(lane0, half)], gathered.at[taps, own, :],
-                w_send.at[slot, k], w_recv.at[slot, k], ((r + k) % R, q, c))
-            for k in range(1, R)
-        ]
-
-    def relays(shard, gathered, slot):
-        rows = shard.shape[1]
-        taps = pl.ds(2 * group * parity, group)
-        other = q + 1 - 2 * parity
+    inner, outer = r % 2, R // 2
+    pair_row, pair_col = r + 1 - 2 * inner, q + 1 - 2 * parity
+    most, rest = pl.ds(group * parity, 2 * group), pl.ds(2 * group * parity, group)
+    part = last_ref.shape[1] // 2
+    blocks = (
+        (first_ref, first_w, 0, first_ref.shape[1]),
+        (last_ref, last_w, 0, part),
+        (last_ref, last_w, part, part),
+    )
+
+    def rows_at(n, origin):
+        shard, _, low, count = blocks[n]
+        return pl.ds(pl.multiple_of(origin * shard.shape[1] + low, count), count)
+
+    def origin_of(k, side):
+        return (r + R - 2 * k) % R - inner + side
+
+    def leg(n, step):
+        shard, gathered, low, count = blocks[n]
+        mine = shard.at[most, pl.ds(low, count), pl.ds(lane0, half)]
         out = []
-        for k in range(1, R):
-            origin = (r + R - k) % R
-            at = pl.ds(pl.multiple_of(origin * rows, rows), rows)
-            out.append(remote(
-                gathered.at[taps, at, :], gathered.at[taps, at, :],
-                relay_send.at[slot, k], relay_recv.at[slot, k], (r, other, c)))
+        if step == 0:
+            at = rows_at(n, r)
+            for k in range(1, outer):
+                out.append(remote(
+                    mine, gathered.at[most, at, :], w_send.at[n, k], w_recv.at[n, k],
+                    ((r + 2 * k) % R, q, c)))
+        elif step == 1:
+            for k in range(outer):
+                at = rows_at(n, origin_of(k, inner))
+                out.append(remote(
+                    mine if k == 0 else gathered.at[most, at, :], gathered.at[most, at, :],
+                    x_send.at[n, k], x_recv.at[n, k], (pair_row, q, c)))
+        else:
+            for slot in range(1, 2 * outer):
+                k, side = slot % outer, (inner if slot < outer else 1 - inner)
+                at = rows_at(n, origin_of(k, side))
+                out.append(remote(
+                    gathered.at[rest, at, :], gathered.at[rest, at, :],
+                    relay_send.at[n, slot], relay_recv.at[n, slot], (r, pair_col, c)))
         return out
 
-    first_out, last_out = spread(first_ref, first_w, 0), spread(last_ref, last_w, 1)
-    first_relay, last_relay = relays(first_ref, first_w, 0), relays(last_ref, last_w, 1)
-    for copy in first_out:
-        copy.start()
+    legs = [[leg(n, step) for step in range(3)] for n in range(3)]
+
+    def go(n, step):
+        first_leg, second_leg, third_leg = legs[n]
+        if step == 0:
+            for copy in first_leg:
+                copy.start()
+        elif step == 1:
+            second_leg[0].start()
+            for k in range(1, outer):
+                first_leg[k - 1].wait_recv()
+                second_leg[k].start()
+        elif step == 2:
+            for k in range(1, outer):
+                third_leg[k - 1].start()
+            for k in range(outer):
+                second_leg[k].wait_recv()
+                third_leg[outer - 1 + k].start()
+        else:
+            for copy in third_leg:
+                copy.wait_recv()
+
+    go(0, 0)
 
     halo(vol_pair.at[c], everything, 0, False)
 
@@ -174,14 +211,12 @@
 
     build_taps(vol_plane, vol_taps, slice(0, C), C)
 
-    for copy, relay in zip(first_out, first_relay):
-        copy.wait_recv()
-        relay.start()
-    for copy in last_out:
-        copy.start()
+    go(0, 1)
+    go(1, 0)
+    go(2, 0)
+    go(0, 2)
     shards[0].wait()
-    for relay in first_relay:
-        relay.wait_recv()
+    go(0, 3)
 
     def conv(taps_ref, weights):
         chans = weights.shape[1]
@@ -207,7 +242,7 @@
     for copy in skips:
         copy.wait_recv()
     upper = pl.ds(C, C)
-    halo(joined, upper, 1, True)
+    go(1, 1)
 
     local[0].wait()
     fine_rows, coarse_rows = hy * ZF, hy * hz
@@ -245,11 +280,14 @@
         else:
             pl.when(to)(copy.start)
     coarse_pad[1:1 + hx, pl.ds(1 + q * hy, hy)] = coarse_own[...]
+    halo(joined, upper, 1, True)
+    go(1, 2)
     for dx, copy, to, come in sends:
         if dx == 0:
             copy.wait_recv()
         else:
             pl.when(come)(copy.wait_recv)
+    go(2, 1)
     build_taps(lambda x: coarse_pad[x].astype(F32), coarse_taps, slice(0, wide), wide)
 
     local[1].wait()
@@ -273,10 +311,7 @@
         copy.start()
     middle_all[q] = middle_out[q]
 
-    for copy, relay in zip(last_out, last_relay):
-        copy.wait_recv()
-        relay.start()
-
+    go(2, 2)
     halo(joined, upper, 1, False)
     for x in range(X + 2):
         v = joined[x, :, :, C:2 * C].astype(F32)
@@ -306,8 +341,8 @@
     lower = pl.ds(0, C)
     halo(joined, lower, 2, True)
     shards[1].wait()
-    for relay in last_relay:
-        relay.wait_recv()
+    go(1, 3)
+    go(2, 3)
     halo(joined, lower, 2, False)
     for x in range(X + 2):
         v = joined[x, :, :, 0:C].astype(F32)
@@ -331,7 +366,7 @@
     for d in range(D):
         out_ref[:, :, :, d * half:(d + 1) * half] = piece_all[d]
 
-    for copy in first_out + last_out + first_relay + last_relay + vols + skips + mids + pieces:
+    for copy in [copy for block in legs for step in block for copy in step] + vols + skips + mids + pieces:
         copy.wait_send()
     for dx, copy, to, come in sends:
         if dx == 0:
@@ -374,7 +409,7 @@
             pltpu.VMEM((D, X, Y, Z, half), BF),
             pltpu.VMEM((D, X, Y, Z, half), BF),
             DMA((5,)),
-            DMA((2, R)), DMA((2, R)), DMA((2, R)), DMA((2, R)),
+            DMA((3, R)), DMA((3, R)), DMA((3, R)), DMA((3, R)), DMA((3, R)), DMA((3, R)),
             DMA((3, 8)), DMA((3, 8)),
             DMA((3, D)), DMA((3, D)),
             DMA((3, Q)), DMA((3, Q)),

time: 125 us -> 93.3 us (0.75)
  the two profiles are of different devices: /device:TPU:15 before, /device:TPU:13 now
where the time goes in v2:
time: 93.3 us; the launch traced here: 93.2 us
  Pallas kernels  91.6 us (98%)
  local copies, waits for them, and re-layouts  1.57 us (2%)
    pallas_call x1, Pallas kernels, body(): pl.pallas_call(functools.partial(kernel, sizes), out_shape=jax.ShapeDtype...  91.6 us

profile of v2, /device:TPU:13, one launch (start us, length us, event | category | flops | bytes accessed | tf_op | source)
XLA Modules:
  0.0 93.2 jit_solution(3773544405779196481)
XLA Ops:
  0.0 91.6 %unet.1 = bf16[2,16,8,256]{3,2,1,0:T(8,128)(2,1)} custom-call(bf16[2,16,8,256]{3,2,1,0:T(8,128)(2,1)} %vol_ref.1, bf16[27,32,256]{2,1,0:T(8,128)(2,1)} %first_ref.1, bf16[8,256,512]{2,1,0:T(8,128)(2,1)} %down_hbm.1, bf16[27,512,256]{2,1,0:T(8,128)(2,1)} %mid_hbm.1, bf16[8,512,256]{2,1,0:T(8,128)(2,1)} %up_hbm.1, bf16[27,64,256]{2,1,0:T(8,128)(2,1)} %last_ref.1), custom_call_target="tpu_custom_call" | custom-call | tf_op jit(solution)/shard_map/unet/pallas_call | solution.py:388
  91.6 1.6 %copy.8 = bf16[2,16,8,256]{3,2,1,0:T(8,128)(2,1)} copy(bf16[2,16,8,256]{3,2,1,0:T(8,128)(2,1)} %unet.1) | data formatting | bytes 262144

commit v3 on v1

--- a/solution.py
+++ b/solution.py
@@ -37,7 +37,7 @@
     vol_pair, vol_taps, first_w, last_w, down_ref, mid_ref, up_ref,
     joined, joined_taps, acc, coarse_pad, coarse_own, coarse_taps,
     middle_out, middle_all, piece_out, piece_all,
-    local_sem, w_send, w_recv, relay_send, relay_recv,
+    local_sem, w_send, w_recv, x_send, x_recv, relay_send, relay_recv,
     halo_send, halo_recv, pair_send, pair_recv,
     coarse_send, coarse_recv, mid_send, mid_recv,
 ):
@@ -122,34 +122,113 @@
     everything = pl.ds(0, C)
     halo(vol_pair.at[c], everything, 0, True)
 
-    def spread(shard, gathered, slot):
-        rows = shard.shape[1]
-        own = pl.ds(pl.multiple_of(r * rows, rows), rows)
-        taps = pl.ds(group * parity, 2 * group)
-        return [
-            remote(
-                shard.at[taps, :, pl.ds(lane0, half)], gathered.at[taps, own, :],
-                w_send.at[slot, k], w_recv.at[slot, k], ((r + k) % R, q, c))
-            for k in range(1, R)
-        ]
-
-    def relays(shard, gathered, slot):
-        rows = shard.shape[1]
-        taps = pl.ds(2 * group * parity, group)
-        other = q + 1 - 2 * parity
-        out = []
-        for k in range(1, R):
-            origin = (r + R - k) % R
-            at = pl.ds(pl.multiple_of(origin * rows, rows), rows)
-            out.append(remote(
-                gathered.at[taps, at, :], gathered.at[taps, at, :],
-                relay_send.at[slot, k], relay_recv.at[slot, k], (r, other, c)))
-        return out
-
-    first_out, last_out = spread(first_ref, first_w, 0), spread(last_ref, last_w, 1)
-    first_relay, last_relay = relays(first_ref, first_w, 0), relays(last_ref, last_w, 1)
-    for copy in first_out:
-        copy.start()
+    inner, outer = r % 2, R // 2
+    pair_row, pair_col = r + 1 - 2 * inner, q + 1 - 2 * parity
+    most, rest = pl.ds(group * parity, 2 * group), pl.ds(2 * group * parity, group)
+    part = last_ref.shape[1] // 2
+    blocks = (
+        (first_ref, first_w, 0, first_ref.shape[1]),
+        (last_ref, last_w, 0, part),
+        (last_ref, last_w, part, part),
+    )
+
+    def rows_at(n, origin):
+        shard, _, low, count = blocks[n]
+        return pl.ds(pl.multiple_of(origin * shard.shape[1] + low, count), count)
+
+    line = r // 2
+
+    def arrives(way, s):
+        return line - 1 - s >= 0 if way == 0 else line + 1 + s < outer
+
+    def leaves(way, s):
+        if way == 0:
+            return (line - s >= 0) & (line + 1 < outer)
+        return (line + s < outer) & (line - 1 >= 0)
+
+    def origin_of(way, s, side):
+        return 2 * (line - 1 - s if way == 0 else line + 1 + s) + side
+
+    def hop(n, way, s):
+        shard, gathered, low, count = blocks[n]
+        origin = origin_of(way, s - 1, inner)
+        at = rows_at(n, jnp.clip(origin, 0, R - 1))
+        src = shard.at[most, pl.ds(low, count), pl.ds(lane0, half)] if s == 0 else (
+            gathered.at[most, at, :])
+        return remote(
+            src, gathered.at[most, at, :], w_send.at[n, 2 * s + way], w_recv.at[n, 2 * s + way],
+            (r + 2 - 4 * way, q, c))
+
+    def across(n, way, s):
+        shard, gathered, low, count = blocks[n]
+        at = rows_at(n, jnp.clip(origin_of(way, s, inner), 0, R - 1))
+        src = shard.at[most, pl.ds(low, count), pl.ds(lane0, half)] if s < 0 else (
+            gathered.at[most, at, :])
+        slot = 2 * s + way + 2
+        return remote(
+            src, gathered.at[most, at, :], x_send.at[n, slot], x_recv.at[n, slot],
+            (pair_row, q, c))
+
+    def over(n, way, s, other):
+        _, gathered, _, _ = blocks[n]
+        side = 1 - inner if other else inner
+        at = rows_at(n, jnp.clip(origin_of(way, s, side), 0, R - 1))
+        slot = 4 * s + 2 * way + other + 4
+        return remote(
+            gathered.at[rest, at, :], gathered.at[rest, at, :],
+            relay_send.at[n, slot], relay_recv.at[n, slot], (r, pair_col, c))
+
+    ways = [(way, s) for s in range(outer - 1) for way in range(2)]
+
+    def begin(n):
+        for way in range(2):
+            pl.when(leaves(way, 0))(hop(n, way, 0).start)
+        across(n, 0, -1).start()
+
+    def forward(n, steps):
+        for s in steps:
+            for way in range(2):
+                @pl.when(arrives(way, s))
+                def _(way=way, s=s):
+                    hop(n, way, s).wait_recv()
+                if s + 1 < outer - 1:
+                    pl.when(leaves(way, s + 1))(hop(n, way, s + 1).start)
+                pl.when(arrives(way, s))(across(n, way, s).start)
+
+    def share(n):
+        for way, s in ways:
+            pl.when(arrives(way, s))(over(n, way, s, 0).start)
+        across(n, 0, -1).wait_recv()
+        over(n, 0, -1, 1).start()
+        for way, s in ways:
+            @pl.when(arrives(way, s))
+            def _(way=way, s=s):
+                across(n, way, s).wait_recv()
+                over(n, way, s, 1).start()
+
+    def finish(n):
+        over(n, 0, -1, 1).wait_recv()
+        for way, s in ways:
+            @pl.when(arrives(way, s))
+            def _(way=way, s=s):
+                over(n, way, s, 0).wait_recv()
+                over(n, way, s, 1).wait_recv()
+
+    def drain(n):
+        across(n, 0, -1).wait_send()
+        over(n, 0, -1, 1).wait_send()
+        for way, s in ways:
+            pl.when(leaves(way, s))(hop(n, way, s).wait_send)
+
+            @pl.when(arrives(way, s))
+            def _(way=way, s=s):
+                across(n, way, s).wait_send()
+                over(n, way, s, 0).wait_send()
+                over(n, way, s, 1).wait_send()
+
+    first_hop, later_hops = range(0, 1), range(1, outer - 1)
+
+    begin(0)
 
     halo(vol_pair.at[c], everything, 0, False)
 
@@ -174,14 +253,14 @@
 
     build_taps(vol_plane, vol_taps, slice(0, C), C)
 
-    for copy, relay in zip(first_out, first_relay):
-        copy.wait_recv()
-        relay.start()
-    for copy in last_out:
-        copy.start()
+    forward(0, first_hop)
+    forward(0, later_hops)
+    begin(1)
+    share(0)
     shards[0].wait()
-    for relay in first_relay:
-        relay.wait_recv()
+    finish(0)
+    forward(1, first_hop)
+    begin(2)
 
     def conv(taps_ref, weights):
         chans = weights.shape[1]
@@ -207,7 +286,7 @@
     for copy in skips:
         copy.wait_recv()
     upper = pl.ds(C, C)
-    halo(joined, upper, 1, True)
+    forward(1, later_hops)
 
     local[0].wait()
     fine_rows, coarse_rows = hy * ZF, hy * hz
@@ -245,11 +324,15 @@
         else:
             pl.when(to)(copy.start)
     coarse_pad[1:1 + hx, pl.ds(1 + q * hy, hy)] = coarse_own[...]
+    halo(joined, upper, 1, True)
+    share(1)
+    forward(2, first_hop)
     for dx, copy, to, come in sends:
         if dx == 0:
             copy.wait_recv()
         else:
             pl.when(come)(copy.wait_recv)
+    forward(2, later_hops)
     build_taps(lambda x: coarse_pad[x].astype(F32), coarse_taps, slice(0, wide), wide)
 
     local[1].wait()
@@ -272,16 +355,6 @@
     for copy in mids:
         copy.start()
     middle_all[q] = middle_out[q]
-
-    for copy, relay in zip(last_out, last_relay):
-        copy.wait_recv()
-        relay.start()
-
-    halo(joined, upper, 1, False)
-    for x in range(X + 2):
-        v = joined[x, :, :, C:2 * C].astype(F32)
-        for s in range(3):
-            joined_taps[x, :, :, s * 2 * C + C:(s + 1) * 2 * C] = z_shifted(v, s - 1).astype(BF)
 
     for copy in mids:
         copy.wait_recv()
@@ -305,9 +378,16 @@
                     joined[1 + 2 * i + a, 1 + 2 * j + b, :, 0:C] = lifted[j * ZF:(j + 1) * ZF]
     lower = pl.ds(0, C)
     halo(joined, lower, 2, True)
+    share(2)
+    halo(joined, upper, 1, False)
+    for x in range(X + 2):
+        v = joined[x, :, :, C:2 * C].astype(F32)
+        for s in range(3):
+            joined_taps[x, :, :, s * 2 * C + C:(s + 1) * 2 * C] = z_shifted(v, s - 1).astype(BF)
+
     shards[1].wait()
-    for relay in last_relay:
-        relay.wait_recv()
+    finish(1)
+    finish(2)
     halo(joined, lower, 2, False)
     for x in range(X + 2):
         v = joined[x, :, :, 0:C].astype(F32)
@@ -331,7 +411,9 @@
     for d in range(D):
         out_ref[:, :, :, d * half:(d + 1) * half] = piece_all[d]
 
-    for copy in first_out + last_out + first_relay + last_relay + vols + skips + mids + pieces:
+    for n in range(3):
+        drain(n)
+    for copy in vols + skips + mids + pieces:
         copy.wait_send()
     for dx, copy, to, come in sends:
         if dx == 0:
@@ -374,7 +456,7 @@
             pltpu.VMEM((D, X, Y, Z, half), BF),
             pltpu.VMEM((D, X, Y, Z, half), BF),
             DMA((5,)),
-            DMA((2, R)), DMA((2, R)), DMA((2, R)), DMA((2, R)),
+            DMA((3, R)), DMA((3, R)), DMA((3, R)), DMA((3, R)), DMA((3, 2 * R)), DMA((3, 2 * R)),
             DMA((3, 8)), DMA((3, 8)),
             DMA((3, D)), DMA((3, D)),
             DMA((3, Q)), DMA((3, Q)),

time: 125 us -> 87.3 us (0.70)
  the two profiles are of different devices: /device:TPU:15 before, /device:TPU:0 now
where the time goes in v3:
time: 87.3 us; the launch traced here: 87 us
  Pallas kernels  85.4 us (98%)
  local copies, waits for them, and re-layouts  1.57 us (2%)
    pallas_call x1, Pallas kernels, body(): pl.pallas_call(functools.partial(kernel, sizes), out_shape=jax.ShapeDtype...  85.4 us

profile of v3, /device:TPU:0, one launch (start us, length us, event | category | flops | bytes accessed | tf_op | source)
XLA Modules:
  0.0 87.0 jit_solution(5527837839947806978)
XLA Ops:
  0.0 85.4 %unet.1 = bf16[2,16,8,256]{3,2,1,0:T(8,128)(2,1)} custom-call(bf16[2,16,8,256]{3,2,1,0:T(8,128)(2,1)} %vol_ref.1, bf16[27,32,256]{2,1,0:T(8,128)(2,1)} %first_ref.1, bf16[8,256,512]{2,1,0:T(8,128)(2,1)} %down_hbm.1, bf16[27,512,256]{2,1,0:T(8,128)(2,1)} %mid_hbm.1, bf16[8,512,256]{2,1,0:T(8,128)(2,1)} %up_hbm.1, bf16[27,64,256]{2,1,0:T(8,128)(2,1)} %last_ref.1), custom_call_target="tpu_custom_call" | custom-call | tf_op jit(solution)/shard_map/unet/pallas_call | solution.py:435
  85.4 1.6 %copy.8 = bf16[2,16,8,256]{3,2,1,0:T(8,128)(2,1)} copy(bf16[2,16,8,256]{3,2,1,0:T(8,128)(2,1)} %unet.1) | data formatting | bytes 262144
